TPU v7x, 32 devices: a whole 2x2x4 slice. The times are simulated.
32 devices in a mesh: real: 2 (over x), bx: 4 (over y, core), by: 4 (over z).
Axes of the slice: x: 2, y: 2, z: 4, core: 2. Of those that a mesh axis runs over, the one named last changes fastest.
Arguments:
- current: float32 [2, 12, 3, 8, 32, 128], P('real', None, None, 'bx', 'by'), may hold values from -110 to 110
- previous: float32 [2, 12, 3, 8, 32, 128], P('real', None, None, 'bx', 'by'), may hold values from -110 to 110
- element_stiffness: float32 [24, 24], replicated, may hold values from -0.75 to 1.25, as said below
- preconditioner: float32 [2, 3, 8, 32, 128], P('real', None, 'bx', 'by'), may hold values from 0.04 to 0.16
- modulus: float32 [8, 32, 128], P('bx', 'by'), may hold values from 0.3 to 9.1
- density: float32 [8, 32, 128], P('bx', 'by'), may hold values from 0.5 to 2
- solid: int32 [2, 8, 32, 128], P('real', 'bx', 'by'), may hold values from 0 to 1, as said below
- clamped: int32 [8, 32], P('bx', 'by'), may hold values 0 or 1
Outputs:
- gram_stiff: float32 [2, 36, 36], P('real')
- gram_mass: float32 [2, 36, 36], P('real')
- search_block: float32 [2, 12, 3, 8, 32, 128], P('real', None, None, 'bx', 'by')
- sensitivity: float32 [8, 32, 128], P('bx', 'by', 'real')
Inputs may be any that keep to these rules, and one draw needn't show every extreme that they name: `element_stiffness`: symmetric positive definite: the stiffness of a trilinear brick of unit edge for unit modulus and a Poisson ratio between 0.25 and 0.35, divided by its diagonal entry, plus a small positive definite part. 1 marks a solid element of that realization; a realization's solid elements include those of every realization before it. `clamped`: 1 marks a bottom-face node held in all three directions.
All inputs are finite; a program needn't handle non-finite values. No bound on the sum of `clamped` on one device may be relied on, other than what follows from the above.
Results may differ from a plain program's by a relative error of at most 0.00013.
Values sent between devices are 32-bit elements; how exact they have to be, the bound alone decides.
No kernel may reach another device: no remote copies, remote signals or barrier semaphores. Data moves between devices by JAX's collectives and lax.ppermute only.
A program may use at most 64 MiB of HBM per device.

v0:
```python
import jax
import jax.numpy as jnp
from jax import lax
from jax.sharding import PartitionSpec as P

highest = lax.Precision.HIGHEST
soft_power = 4.0
group_width = 4
corner_list = [
    (0, 0, 0),
    (0, 0, 1),
    (0, 1, 0),
    (0, 1, 1),
    (1, 0, 0),
    (1, 0, 1),
    (1, 1, 0),
    (1, 1, 1),
]


def from_behind(value, axis, steps):
    count = lax.axis_size(axis)
    leading, last = (max(0, -steps), min(count, count - steps))
    return lax.ppermute(value, axis, [(source, source + steps) for source in range(leading, last)])


def corner_values(extended, size_x, size_y, size_z):
    return jnp.stack(
        [
            extended[
                ...,
                shift_x : shift_x + size_x,
                shift_y : shift_y + size_y,
                shift_z : shift_z + size_z,
            ]
            for shift_x, shift_y, shift_z in corner_list
        ],
        0,
    )


def scatter_corners(pieces):
    leading = pieces.ndim - 4
    overall = 0.0
    for corner, (shift_x, shift_y, shift_z) in enumerate(corner_list):
        widths = [(0, 0)] * leading + [
            (shift_x, 1 - shift_x),
            (shift_y, 1 - shift_y),
            (shift_z, 1 - shift_z),
        ]
        overall = overall + jnp.pad(pieces[corner], widths)
    return overall


def element_pass(extended, stiff_field, element_four):
    size_x, size_y, size_z = stiff_field.shape
    corner_vals = corner_values(extended, size_x, size_y, size_z)
    forces = jnp.einsum("adbe,bkexyz->akdxyz", element_four, corner_vals, precision=highest)
    energy_stiff = jnp.einsum("akdxyz,akdxyz->kxyz", corner_vals, forces, precision=highest)
    energy_mass = jnp.sum(corner_vals * corner_vals, axis=(0, 2)) * 0.125
    return (scatter_corners(forces * stiff_field), energy_stiff, energy_mass)


def grouped_pass(extended, stiff_field, element_four):
    columns = extended.shape[0]
    groups = extended.reshape((columns // group_width, group_width) + extended.shape[1:])

    def run_group(group_block):
        return element_pass(group_block, stiff_field, element_four)

    assembled, energy_stiff, energy_mass = lax.map(run_group, groups)
    return (
        assembled.reshape((columns,) + assembled.shape[2:]),
        energy_stiff.reshape((columns,) + energy_stiff.shape[2:]),
        energy_mass.reshape((columns,) + energy_mass.shape[2:]),
    )


def apply_block(block, stiff_field, free_mask, element_four):
    size_x, size_y, size_z = stiff_field.shape
    upper_rim = from_behind(block[:, :, :, 0:1], "by", -1)
    widened = jnp.concatenate([block, upper_rim], 3)
    beside = from_behind(widened[:, :, 0:1], "bx", -1)
    widened = jnp.concatenate([widened, beside], 2)
    extended = jnp.pad(widened, ((0, 0), (0, 0), (0, 0), (0, 0), (0, 1)))
    assembled, energy_stiff, energy_mass = grouped_pass(extended, stiff_field, element_four)
    assembled = assembled[..., :size_z]
    spill_first = from_behind(assembled[:, :, size_x:], "bx", 1)
    owned_part = jnp.concatenate([assembled[:, :, 0:1] + spill_first, assembled[:, :, 1:size_x]], 2)
    spill_second = from_behind(owned_part[:, :, :, size_y:], "by", 1)
    owned_part = jnp.concatenate(
        [owned_part[:, :, :, 0:1] + spill_second, owned_part[:, :, :, 1:size_y]], 3
    )
    return (owned_part * free_mask, energy_stiff, energy_mass)


def lumped_nodes(mass_rims, size_x, size_y, size_z):
    return scatter_corners(jnp.stack([mass_rims] * 8, 0))[1 : size_x + 1, 1 : size_y + 1, :size_z]


def column_dots(left_block, right_block):
    return jnp.sum(left_block * right_block, axis=(1, 2, 3, 4))


def gram_matrix(left_blocks, right_blocks):
    gram_rows = []
    for left_block in left_blocks:
        flat_left = left_block.reshape(left_block.shape[0], -1)
        gram_rows.append(
            jnp.concatenate(
                [
                    jnp.einsum(
                        "ik,jk->ij",
                        flat_left,
                        right_block.reshape(right_block.shape[0], -1),
                        precision=highest,
                    )
                    for right_block in right_blocks
                ],
                1,
            )
        )
    return jnp.concatenate(gram_rows, 0)


def shards(current, previous, element_stiffness, preconditioner, modulus, density, solid, clamped):
    element_four = element_stiffness.reshape(8, 3, 8, 3)
    size_x, size_y, size_z = modulus.shape
    columns = current.shape[1]
    dof_count = 3.0 * size_x * size_y * size_z * lax.axis_size("bx") * lax.axis_size("by")
    bottom = (jnp.arange(size_z) == 0).astype(jnp.float32)
    free_mask = 1.0 - clamped.astype(jnp.float32)[:, :, None] * bottom
    solid_share = solid[0].astype(jnp.float32)
    stiff_field = modulus * (0.02 + 0.98 * solid_share)
    mass_field = density * (0.1 + 0.9 * solid_share)
    mass_eighth = mass_field * 0.125
    below_x = from_behind(mass_eighth[size_x - 1 :], "bx", 1)
    widened_mass = jnp.concatenate([below_x, mass_eighth], 0)
    below_y = from_behind(widened_mass[:, size_y - 1 :], "by", 1)
    mass_rims = jnp.concatenate([below_y, widened_mass], 1)
    lumped_free = lumped_nodes(mass_rims, size_x, size_y, size_z) * free_mask
    current_free = current[0] * free_mask
    previous_free = previous[0] * free_mask
    stiff_pair, energy_stiff, energy_mass = apply_block(
        jnp.concatenate([current_free, previous_free], 0), stiff_field, free_mask, element_four
    )
    stiff_cur = stiff_pair[:columns]
    stiff_prev = stiff_pair[columns:]
    mass_cur = lumped_free * current_free
    mass_prev = lumped_free * previous_free
    energy_stiff = energy_stiff[:columns]
    energy_mass = energy_mass[:columns]
    scaling = preconditioner[0][None]
    numerator, denominator = lax.psum(
        (
            column_dots(current_free, stiff_cur) / dof_count,
            column_dots(current_free, mass_cur) / dof_count,
        ),
        ("bx", "by"),
    )
    quotient = numerator / denominator
    search = scaling * (stiff_cur - mass_cur * quotient[:, None, None, None, None])
    stiff_search, _, _ = apply_block(search, stiff_field, free_mask, element_four)
    mass_search = lumped_free * search
    search_basis = [current_free, search, previous_free]
    gram_stiff, gram_mass = lax.psum(
        (
            gram_matrix(search_basis, [stiff_cur, stiff_search, stiff_prev]) / dof_count,
            gram_matrix(search_basis, [mass_cur, mass_search, mass_prev]) / dof_count,
        ),
        ("bx", "by"),
    )
    powered = quotient ** (-soft_power)
    overall = lax.psum(jnp.sum(powered), "real")
    coefficient = powered / denominator
    local_terms = 3.0 * stiff_field * jnp.einsum(
        "j,jxyz->xyz", coefficient, energy_stiff, precision=highest
    ) - mass_field * jnp.einsum(
        "j,jxyz->xyz", coefficient * quotient, energy_mass, precision=highest
    )
    summed = lax.psum_scatter(local_terms, "real", scatter_dimension=2, tiled=True)
    sensitivity = summed / overall
    return (gram_stiff[None], gram_mass[None], search[None], sensitivity)


def solution(mesh):
    in_specs = (
        P("real", None, None, "bx", "by", None),
        P("real", None, None, "bx", "by", None),
        P(),
        P("real", None, "bx", "by", None),
        P("bx", "by", None),
        P("bx", "by", None),
        P("real", "bx", "by", None),
        P("bx", "by"),
    )
    out_specs = (
        P("real", None, None),
        P("real", None, None),
        P("real", None, None, "bx", "by", None),
        P("bx", "by", "real"),
    )
    return jax.shard_map(shards, mesh=mesh, in_specs=in_specs, out_specs=out_specs, check_vma=False)
```

profile of v0, /device:TPU:0, one launch (start us, length us, event | category | flops | bytes accessed | tf_op | source)
XLA Modules:
  0.0 269.4 jit_solution(3262459947060934971)
XLA Ops:
  8.0 2.4 collective-permute-start.4
  11.2 4.4 %collective-permute-start.5 = (f32[3,1,128]{2,1,0:T(1,128)S(1)}, f32[3,1,128]{2,1,0:T(1,128)S(1)}, u32[]{:S(2)}, u32[]{:S(2)}) collective-permute-start(f32[3,1,128]{2,1,0:T(1,128)S(1)} %pad_maximum_fusion.8), channel_id=1, source_target_pairs={{0,1},{1,2},{2,3},{4,5},{5,6},{6,7},{8,9},{9,10},{10,11},{12,13},{... | collective-permute-start | bytes 4616 | tf_op jit(solution)/shard_map/ppermute | solution.py:24
  19.6 5.9 %collective-permute-done = f32[24,3,2,1,128]{4,0,3,2,1:T(8,128)S(1)} collective-permute-done((f32[24,3,2,1,128]{4,0,3,2,1:T(8,128)S(1)}, f32[24,3,2,1,128]{4,0,3,2,1:T(8,128)S(1)}, u32[]{:S(2)}, u32[]{:S(2)}) %collective-permute-start) | collective-permute-done | bytes 73760 | tf_op jit(solution)/shard_map/ppermute | solution.py:24
  29.5 2.2 pad.144.clone
  31.7 45.1 %while.28 = (s32[]{:T(128)}, f32[6,4,3,3,9,129]{5,4,3,2,1,0:T(8,128)}, f32[6,4,2,8,128]{4,3,2,1,0:T(8,128)S(1)}, f32[6,4,2,8,128]{4,3,2,1,0:T(8,128)}, f32[6,4,3...) while((s32[]{:T(128)}, ...), condition=%wide.region_2.3_spmd, body=%wide.region_0.2_spmd.sunk | while | flops 57890524 | bytes 14501753 | solution.py:71
  33.9 1.7 stack.110
  41.4 1.7 stack.110
  48.9 1.7 stack.110
  56.4 1.7 stack.110
  64.0 1.7 stack.110
  71.5 1.7 stack.110
  76.8 1.7 fusion.61
  78.6 8.4 %collective-permute-start.2 = (f32[24,3,1,9,128]{4,0,3,2,1:T(8,128)S(1)}, f32[24,3,1,9,128]{4,0,3,2,1:T(8,128)S(1)}, u32[]{:S(2)}, u32[]{:S(2)}) collective-permute-start(f32[24,3,1,9,128]{4,0,3,2,1:T(8,128)S(1)} %copy.643), channel_id=1, source_target_pairs={{0,4},{4,8},{8,12},{1,5},{5,9},{9,13},{2,6},{6,10},{10,14},{3,7},{... | collective-permute-start | bytes 995336 | tf_op jit(solution)/shard_map/ppermute | solution.py:24
  91.4 3.9 %collective-permute-start.3 = (f32[24,3,2,1,128]{4,0,3,2,1:T(8,128)S(1)}, f32[24,3,2,1,128]{4,0,3,2,1:T(8,128)S(1)}, u32[]{:S(2)}, u32[]{:S(2)}) collective-permute-start(f32[24,3,2,1,128]{4,0,3,2,1:T(8,128)S(1)} %pad_maximum_fusion.5), channel_id=1, source_target_pairs={{0,1},{1,2},{2,3},{4,5},{5,6},{6,7},{8,9},{9,10},{10,11},{12,13},{... | collective-permute-start | bytes 221192 | tf_op jit(solution)/shard_map/ppermute | solution.py:24
  97.6 32.3 %all-reduce.27 = (f32[12]{0:T(128)S(1)}, f32[12]{0:T(128)S(1)}) all-reduce(f32[12]{0:T(128)S(1)} %get-tuple-element.427, f32[12]{0:T(128)S(1)} %get-tuple-element.426), channel_id=1, replica_groups=mesh['real'=2,'bx'=4,'by'=4] {'bx','by'}, use_global_device_ids=true, to_apply=%region_4.5 | all-reduce | flops 24 | bytes 192 | tf_op jit(solution)/shard_map/psum | solution.py:154
  143.0 2.8 %collective-permute-done.6 = f32[12,3,2,1,128]{4,0,3,2,1:T(8,128)S(1)} collective-permute-done((f32[12,3,2,1,128]{4,0,3,2,1:T(8,128)S(1)}, f32[12,3,2,1,128]{4,0,3,2,1:T(8,128)S(1)}, u32[]{:S(2)}, u32[]{:S(2)}) %collective-permute-start.6) | collective-permute-done | bytes 36896 | tf_op jit(solution)/shard_map/ppermute | solution.py:24
  150.1 25.6 %while.29 = (s32[]{:T(128)}, f32[3,4,3,3,9,129]{5,4,3,2,1,0:T(8,128)}, f32[3,4,3,3,9,129]{5,4,3,2,1,0:T(8,128)S(1)}, f32[8,3,8,3]{2,0,3,1:T(8,128)}, f32[2,8,128]{2,1,0:T(8,128)S(1)}, /*index=5*/s32[]{:T(128)}) while((s32[]{:T(128)}, f32[3,4,3,3,9,129]{5,4,3,2,1,0:T(8,128)}, f32[3,4,3,3,9,129]{5,4,3,2,1,0:T(8,128)S(1)}, ...), condition=%wide.region_8.9_spmd, body=%wide.region_7.8_spmd.sunk | while | flops 57112284 | bytes 15171361 | solution.py:71
  152.6 2.4 stack.111
  161.1 2.4 stack.111
  169.6 2.4 stack.111
  177.2 5.9 %collective-permute-start.8 = (f32[12,3,1,9,128]{4,0,3,2,1:T(8,128)S(1)}, f32[12,3,1,9,128]{4,0,3,2,1:T(8,128)S(1)}, u32[]{:S(2)}, u32[]{:S(2)}) collective-permute-start(f32[12,3,1,9,128]{4,0,3,2,1:T(8,128)S(1)} %copy.646), channel_id=1, source_target_pairs={{0,4},{4,8},{8,12},{1,5},{5,9},{9,13},{2,6},{6,10},{10,14},{3,7},{... | collective-permute-start | bytes 497672 | tf_op jit(solution)/shard_map/ppermute | solution.py:24
  184.9 5.5 %psum.39 = f32[]{:T(128)} all-reduce(f32[]{:T(128)} %get-tuple-element.354), channel_id=1, replica_groups=mesh['real'=2,'bx'=4,'by'=4] {'real'}, use_global_device_ids=true, to_apply=%region_13.14 | all-reduce | flops 1 | bytes 8 | tf_op jit(solution)/shard_map/psum | solution.py:174
  193.2 3.4 %collective-permute-start.9 = (f32[12,3,2,1,128]{4,0,3,2,1:T(8,128)S(1)}, f32[12,3,2,1,128]{4,0,3,2,1:T(8,128)S(1)}, u32[]{:S(2)}, u32[]{:S(2)}) collective-permute-start(f32[12,3,2,1,128]{4,0,3,2,1:T(8,128)S(1)} %pad_maximum_fusion.7), channel_id=1, source_target_pairs={{0,1},{1,2},{2,3},{4,5},{5,6},{6,7},{8,9},{9,10},{10,11},{12,13},{... | collective-permute-start | bytes 110600 | tf_op jit(solution)/shard_map/ppermute | solution.py:24
  200.5 60.8 %all-reduce.26 = (f32[1,36,36]{2,1,0:T(8,128)S(1)}, f32[1,36,36]{2,1,0:T(8,128)S(1)}) all-reduce(f32[1,36,36]{2,1,0:T(8,128)S(1)} %fusion.43, f32[1,36,36]{2,1,0:T(8,128)S(1)} %fusion.44), channel_id=1, replica_groups=mesh['real'=2,'bx'=4,'by'=4] {'bx','by'}, use_global_device_ids=true, to_apply=%region_9.10 | all-reduce | flops 2592 | bytes 20736 | tf_op jit(solution)/shard_map/psum | solution.py:166
  (325 shorter events, 96.3 us)
Async XLA Ops:
  7.2 185.0 %reduce-scatter.4.cloned.1.call-start = ((), (), s32[]{:S(2)}) async-start(), calls=%async_computation.1 | async-start | bytes 98304
  8.0 3.2 %collective-permute-start.4 = (f32[1,8,128]{2,1,0:T(8,128)S(1)}, f32[1,8,128]{2,1,0:T(8,128)S(1)}, u32[]{:S(2)}, u32[]{:S(2)}) collective-permute-start(f32[1,8,128]{2,1,0:T(8,128)S(1)} %slice.336), channel_id=1, source_target_pairs={{0,4},{4,8},{8,12},{1,5},{5,9},{9,13},{2,6},{6,10},{10,14},{3,7},{... | collective-permute-start | bytes 12296 | tf_op jit(solution)/shard_map/ppermute | solution.py:24
  11.2 15.7 %copy-start.28 = (f32[24,24]{1,0:T(8,128)S(1)}, f32[24,24]{1,0:T(8,128)}, u32[]{:S(2)}) copy-start(f32[24,24]{1,0:T(8,128)} %param.14) | copy-start | bytes 6916
  11.2 5.7 %collective-permute-start.5 = (f32[3,1,128]{2,1,0:T(1,128)S(1)}, f32[3,1,128]{2,1,0:T(1,128)S(1)}, u32[]{:S(2)}, u32[]{:S(2)}) collective-permute-start(f32[3,1,128]{2,1,0:T(1,128)S(1)} %pad_maximum_fusion.8), channel_id=1, source_target_pairs={{0,1},{1,2},{2,3},{4,5},{5,6},{6,7},{8,9},{9,10},{10,11},{12,13},{... | collective-permute-start | bytes 4616 | tf_op jit(solution)/shard_map/ppermute | solution.py:24
  17.0 10.2 %copy-start = (f32[1,12,3,2,8,128]{5,4,3,2,1,0:T(8,128)S(1)}, f32[1,12,3,2,8,128]{5,4,3,2,1,0:T(8,128)}, u32[]{:S(2)}) copy-start(f32[1,12,3,2,8,128]{5,4,3,2,1,0:T(8,128)} %param.12) | copy-start | bytes 884740
  17.0 10.2 %copy-start.1 = (f32[1,12,3,2,8,128]{5,4,3,2,1,0:T(8,128)S(1)}, f32[1,12,3,2,8,128]{5,4,3,2,1,0:T(8,128)}, u32[]{:S(2)}) copy-start(f32[1,12,3,2,8,128]{5,4,3,2,1,0:T(8,128)} %param.13) | copy-start | bytes 884740
  18.3 7.2 %collective-permute-start = (f32[24,3,2,1,128]{4,0,3,2,1:T(8,128)S(1)}, f32[24,3,2,1,128]{4,0,3,2,1:T(8,128)S(1)}, u32[]{:S(2)}, u32[]{:S(2)}) collective-permute-start(f32[24,3,2,1,128]{4,0,3,2,1:T(8,128)S(1)} %pad_maximum_fusion.6), channel_id=1, source_target_pairs={{1,0},{2,1},{3,2},{5,4},{6,5},{7,6},{9,8},{10,9},{11,10},{13,12},{... | collective-permute-start | bytes 221192 | tf_op jit(solution)/shard_map/ppermute | solution.py:24
  25.6 3.5 %collective-permute-start.1 = (f32[24,3,1,9,128]{4,0,3,2,1:T(8,128)S(1)}, f32[24,3,1,9,128]{4,0,3,2,1:T(8,128)S(1)}, u32[]{:S(2)}, u32[]{:S(2)}) collective-permute-start(f32[24,3,1,9,128]{4,0,3,2,1:T(8,128)S(1)} %pad_maximum_fusion.2), channel_id=1, source_target_pairs={{4,0},{8,4},{12,8},{5,1},{9,5},{13,9},{6,2},{10,6},{14,10},{7,3},{... | collective-permute-start | bytes 995336 | tf_op jit(solution)/shard_map/ppermute | solution.py:24
  76.8 10.3 %copy-start.5 = (f32[12,3,2,8,128]{4,3,2,1,0:T(8,128)S(1)}, f32[12,3,2,8,128]{4,3,2,1,0:T(8,128)}, u32[]{:S(2)}) copy-start(f32[12,3,2,8,128]{4,3,2,1,0:T(8,128)} %get-tuple-element.417) | copy-start | bytes 884740
  78.6 12.6 %collective-permute-start.2 = (f32[24,3,1,9,128]{4,0,3,2,1:T(8,128)S(1)}, f32[24,3,1,9,128]{4,0,3,2,1:T(8,128)S(1)}, u32[]{:S(2)}, u32[]{:S(2)}) collective-permute-start(f32[24,3,1,9,128]{4,0,3,2,1:T(8,128)S(1)} %copy.643), channel_id=1, source_target_pairs={{0,4},{4,8},{8,12},{1,5},{5,9},{9,13},{2,6},{6,10},{10,14},{3,7},{... | collective-permute-start | bytes 995336 | tf_op jit(solution)/shard_map/ppermute | solution.py:24
  91.4 5.9 %collective-permute-start.3 = (f32[24,3,2,1,128]{4,0,3,2,1:T(8,128)S(1)}, f32[24,3,2,1,128]{4,0,3,2,1:T(8,128)S(1)}, u32[]{:S(2)}, u32[]{:S(2)}) collective-permute-start(f32[24,3,2,1,128]{4,0,3,2,1:T(8,128)S(1)} %pad_maximum_fusion.5), channel_id=1, source_target_pairs={{0,1},{1,2},{2,3},{4,5},{5,6},{6,7},{8,9},{9,10},{10,11},{12,13},{... | collective-permute-start | bytes 221192 | tf_op jit(solution)/shard_map/ppermute | solution.py:24
  96.6 34.0 %copy-start.27 = (f32[1,3,2,8,128]{4,3,2,1,0:T(8,128)S(1)}, f32[1,3,2,8,128]{4,3,2,1,0:T(8,128)}, u32[]{:S(2)}) copy-start(f32[1,3,2,8,128]{4,3,2,1,0:T(8,128)} %param.15) | copy-start | bytes 73732
  139.9 6.0 %collective-permute-start.6 = (f32[12,3,2,1,128]{4,0,3,2,1:T(8,128)S(1)}, f32[12,3,2,1,128]{4,0,3,2,1:T(8,128)S(1)}, u32[]{:S(2)}, u32[]{:S(2)}) collective-permute-start(f32[12,3,2,1,128]{4,0,3,2,1:T(8,128)S(1)} %slice.339), channel_id=1, source_target_pairs={{1,0},{2,1},{3,2},{5,4},{6,5},{7,6},{9,8},{10,9},{11,10},{13,12},{... | collective-permute-start | bytes 110600 | tf_op jit(solution)/shard_map/ppermute | solution.py:24
  145.9 3.8 %collective-permute-start.7 = (f32[12,3,1,9,128]{4,0,3,2,1:T(8,128)S(1)}, f32[12,3,1,9,128]{4,0,3,2,1:T(8,128)S(1)}, u32[]{:S(2)}, u32[]{:S(2)}) collective-permute-start(f32[12,3,1,9,128]{4,0,3,2,1:T(8,128)S(1)} %pad_maximum_fusion.4), channel_id=1, source_target_pairs={{4,0},{8,4},{12,8},{5,1},{9,5},{13,9},{6,2},{10,6},{14,10},{7,3},{... | collective-permute-start | bytes 497672 | tf_op jit(solution)/shard_map/ppermute | solution.py:24
  175.8 8.9 %copy-start.10 = (f32[12,12]{1,0:T(8,128)S(1)}, f32[12,12]{1,0:T(8,128)}, u32[]{:S(2)}) copy-start(f32[12,12]{1,0:T(8,128)} %convolution_bitcast_fusion.3) | copy-start | bytes 1732
  175.8 9.0 %copy-start.11 = (f32[12,12]{1,0:T(8,128)S(1)}, f32[12,12]{1,0:T(8,128)}, u32[]{:S(2)}) copy-start(f32[12,12]{1,0:T(8,128)} %convolution_bitcast_fusion.7) | copy-start | bytes 1732
  175.8 9.0 %copy-start.14 = (f32[12,12]{1,0:T(8,128)S(1)}, f32[12,12]{1,0:T(8,128)}, u32[]{:S(2)}) copy-start(f32[12,12]{1,0:T(8,128)} %convolution_bitcast_fusion.9) | copy-start | bytes 1732
  175.8 9.0 %copy-start.18 = (f32[12,12]{1,0:T(8,128)S(1)}, f32[12,12]{1,0:T(8,128)}, u32[]{:S(2)}) copy-start(f32[12,12]{1,0:T(8,128)} %convolution_bitcast_fusion.2) | copy-start | bytes 1732
  175.8 9.0 %copy-start.19 = (f32[12,12]{1,0:T(8,128)S(1)}, f32[12,12]{1,0:T(8,128)}, u32[]{:S(2)}) copy-start(f32[12,12]{1,0:T(8,128)} %convolution_bitcast_fusion.4) | copy-start | bytes 1732
  175.8 9.0 %copy-start.20 = (f32[12,12]{1,0:T(8,128)S(1)}, f32[12,12]{1,0:T(8,128)}, u32[]{:S(2)}) copy-start(f32[12,12]{1,0:T(8,128)} %convolution_bitcast_fusion.6) | copy-start | bytes 1732
  175.8 9.0 %copy-start.21 = (f32[12,12]{1,0:T(8,128)S(1)}, f32[12,12]{1,0:T(8,128)}, u32[]{:S(2)}) copy-start(f32[12,12]{1,0:T(8,128)} %convolution_bitcast_fusion.8) | copy-start | bytes 1732
  175.8 9.0 %copy-start.22 = (f32[12,12]{1,0:T(8,128)S(1)}, f32[12,12]{1,0:T(8,128)}, u32[]{:S(2)}) copy-start(f32[12,12]{1,0:T(8,128)} %convolution_bitcast_fusion.5) | copy-start | bytes 1732
  177.2 15.9 %collective-permute-start.8 = (f32[12,3,1,9,128]{4,0,3,2,1:T(8,128)S(1)}, f32[12,3,1,9,128]{4,0,3,2,1:T(8,128)S(1)}, u32[]{:S(2)}, u32[]{:S(2)}) collective-permute-start(f32[12,3,1,9,128]{4,0,3,2,1:T(8,128)S(1)} %copy.646), channel_id=1, source_target_pairs={{0,4},{4,8},{8,12},{1,5},{5,9},{9,13},{2,6},{6,10},{10,14},{3,7},{... | collective-permute-start | bytes 497672 | tf_op jit(solution)/shard_map/ppermute | solution.py:24
  193.2 5.1 %collective-permute-start.9 = (f32[12,3,2,1,128]{4,0,3,2,1:T(8,128)S(1)}, f32[12,3,2,1,128]{4,0,3,2,1:T(8,128)S(1)}, u32[]{:S(2)}, u32[]{:S(2)}) collective-permute-start(f32[12,3,2,1,128]{4,0,3,2,1:T(8,128)S(1)} %pad_maximum_fusion.7), channel_id=1, source_target_pairs={{0,1},{1,2},{2,3},{4,5},{5,6},{6,7},{8,9},{9,10},{10,11},{12,13},{... | collective-permute-start | bytes 110600 | tf_op jit(solution)/shard_map/ppermute | solution.py:24
  (20 other events, 72.0 us)
Sparse Core Ops, SparseCore 0:
  184.8 7.2 reduce-scatter.3
where the time goes:
time: 271 us; the launch traced here: 269 us
  blocking collectives  98.6 us (36%)
  local copies, waits for them, and re-layouts  53.7 us (20%)
  starting transfers between devices  33.7 us (12%)
  matrix products  30.4 us (11%)
  other arithmetic  24 us (9%)
  between operations  14.6 us (5%)
  waiting for transfers between devices  13.2 us (5%)
    psum x1, blocking collectives, shards(): lax.psum((gram_matrix(search_basis, [stiff_cur, stiff_search, stiff_prev]...  60.8 us
    ppermute x10, starting transfers between devices, from_behind(): lax.ppermute(value, axis, [(source, source + steps) for source in range(l...  33.7 us
    psum x1, blocking collectives, shards(): lax.psum((column_dots(current_free, stiff_cur) / dof_count, column_dots(c...  32.3 us
    another operation x90, local copies, waits for them, and re-layouts, corner_values(): jnp.stack([extended[..., shift_x:shift_x + size_x, shift_y:shift_y + size...  30.4 us
    dot_general x18, matrix products, gram_matrix(): jnp.einsum('ik,jk->ij', flat_left, right_block.reshape(right_block.shape[...  20.3 us
    dynamic_update_slice x15, other arithmetic, grouped_pass(): assembled, energy_stiff, energy_mass = lax.map(run_group, groups)  14.7 us
    ppermute x10, waiting for transfers between devices, from_behind(): lax.ppermute(value, axis, [(source, source + steps) for source in range(l...  12.2 us
    dot_general x9, matrix products, element_pass(): jnp.einsum('adbe,bkexyz->akdxyz', element_four, corner_vals, precision=hi...  9.7 us
  transfers between devices with their start and end apart: 11, of which 8 were waited for; matrix products, arithmetic and copies ran while one was open for 6% of the time, Pallas kernels for 0%

commit v1 on v0

--- a/solution.py
+++ b/solution.py
@@ -152,11 +152,14 @@
     energy_mass = energy_mass[:columns]
     scaling = preconditioner[0][None]
     numerator, denominator = lax.psum(
-        (
-            column_dots(current_free, stiff_cur) / dof_count,
-            column_dots(current_free, mass_cur) / dof_count,
+        lax.psum(
+            (
+                column_dots(current_free, stiff_cur) / dof_count,
+                column_dots(current_free, mass_cur) / dof_count,
+            ),
+            "by",
         ),
-        ("bx", "by"),
+        "bx",
     )
     quotient = numerator / denominator
     search = scaling * (stiff_cur - mass_cur * quotient[:, None, None, None, None])

time: 271 us -> 256 us (0.945)
  blocking collectives: 98.6 us -> 83.5 us
    psum x1, blocking collectives: 32.3 us -> 11.3 us  [shards(): lax.psum((column_dots(current_free, stiff_cur) / dof_count, column_dots(c...]
    psum x0 -> x1, blocking collectives: none -> 5.9 us  [shards(): lax.psum(lax.psum((column_dots(current_free, stiff_cur) / dof_count, colu...]
where the time goes in v1:
time: 256 us; the launch traced here: 254 us
  blocking collectives  83.5 us (33%)
  local copies, waits for them, and re-layouts  53.6 us (21%)
  starting transfers between devices  33.8 us (13%)
  matrix products  30.4 us (12%)
  other arithmetic  23.4 us (9%)
  between operations  14.6 us (6%)
  waiting for transfers between devices  13.9 us (5%)
    psum x1, blocking collectives, shards(): lax.psum((gram_matrix(search_basis, [stiff_cur, stiff_search, stiff_prev]...  60.8 us
    ppermute x10, starting transfers between devices, from_behind(): lax.ppermute(value, axis, [(source, source + steps) for source in range(l...  33.7 us
    another operation x90, local copies, waits for them, and re-layouts, corner_values(): jnp.stack([extended[..., shift_x:shift_x + size_x, shift_y:shift_y + size...  30.4 us
    dot_general x18, matrix products, gram_matrix(): jnp.einsum('ik,jk->ij', flat_left, right_block.reshape(right_block.shape[...  20.3 us
    dynamic_update_slice x15, other arithmetic, grouped_pass(): assembled, energy_stiff, energy_mass = lax.map(run_group, groups)  14.8 us
    ppermute x10, waiting for transfers between devices, from_behind(): lax.ppermute(value, axis, [(source, source + steps) for source in range(l...  12.9 us
    psum x1, blocking collectives, shards(): lax.psum((column_dots(current_free, stiff_cur) / dof_count, column_dots(c...  11.3 us
    dot_general x9, matrix products, element_pass(): jnp.einsum('adbe,bkexyz->akdxyz', element_four, corner_vals, precision=hi...  9.7 us
  transfers between devices with their start and end apart: 11, of which 8 were waited for; matrix products, arithmetic and copies ran while one was open for 6% of the time, Pallas kernels for 0%

profile of v1, /device:TPU:0, one launch (start us, length us, event | category | flops | bytes accessed | tf_op | source)
XLA Modules:
  0.0 254.4 jit_solution(9586540628312585634)
XLA Ops:
  8.0 2.4 collective-permute-start.4
  11.2 4.4 %collective-permute-start.5 = (f32[3,1,128]{2,1,0:T(1,128)S(1)}, f32[3,1,128]{2,1,0:T(1,128)S(1)}, u32[]{:S(2)}, u32[]{:S(2)}) collective-permute-start(f32[3,1,128]{2,1,0:T(1,128)S(1)} %pad_maximum_fusion.8), channel_id=1, source_target_pairs={{0,1},{1,2},{2,3},{4,5},{5,6},{6,7},{8,9},{9,10},{10,11},{12,13},{... | collective-permute-start | bytes 4616 | tf_op jit(solution)/shard_map/ppermute | solution.py:24
  19.6 5.9 %collective-permute-done = f32[24,3,2,1,128]{4,0,3,2,1:T(8,128)S(1)} collective-permute-done((f32[24,3,2,1,128]{4,0,3,2,1:T(8,128)S(1)}, f32[24,3,2,1,128]{4,0,3,2,1:T(8,128)S(1)}, u32[]{:S(2)}, u32[]{:S(2)}) %collective-permute-start) | collective-permute-done | bytes 73760 | tf_op jit(solution)/shard_map/ppermute | solution.py:24
  27.3 1.8 collective-permute-done.1
  29.5 2.2 pad.144.clone
  31.7 45.2 %while.28 = (s32[]{:T(128)}, f32[6,4,3,3,9,129]{5,4,3,2,1,0:T(8,128)}, f32[6,4,2,8,128]{4,3,2,1,0:T(8,128)}, f32[6,4,2,8,128]{4,3,2,1,0:T(8,128)}, f32[6,4,3,3,9...) while((s32[]{:T(128)}, ...), condition=%wide.region_2.3_spmd, body=%wide.region_0.2_spmd.sunk | while | flops 57890524 | bytes 14501753 | solution.py:71
  33.9 1.7 stack.110
  41.4 1.7 stack.110
  48.9 1.7 stack.110
  56.5 1.7 stack.110
  64.0 1.7 stack.110
  78.6 8.4 %collective-permute-start.2 = (f32[24,3,1,9,128]{4,0,3,2,1:T(8,128)S(1)}, f32[24,3,1,9,128]{4,0,3,2,1:T(8,128)S(1)}, u32[]{:S(2)}, u32[]{:S(2)}) collective-permute-start(f32[24,3,1,9,128]{4,0,3,2,1:T(8,128)S(1)} %copy.643), channel_id=1, source_target_pairs={{0,4},{4,8},{8,12},{1,5},{5,9},{9,13},{2,6},{6,10},{10,14},{3,7},{... | collective-permute-start | bytes 995336 | tf_op jit(solution)/shard_map/ppermute | solution.py:24
  91.3 3.9 %collective-permute-start.3 = (f32[24,3,2,1,128]{4,0,3,2,1:T(8,128)S(1)}, f32[24,3,2,1,128]{4,0,3,2,1:T(8,128)S(1)}, u32[]{:S(2)}, u32[]{:S(2)}) collective-permute-start(f32[24,3,2,1,128]{4,0,3,2,1:T(8,128)S(1)} %pad_maximum_fusion.5), channel_id=1, source_target_pairs={{0,1},{1,2},{2,3},{4,5},{5,6},{6,7},{8,9},{9,10},{10,11},{12,13},{... | collective-permute-start | bytes 221192 | tf_op jit(solution)/shard_map/ppermute | solution.py:24
  97.6 11.3 %all-reduce.27 = (f32[12]{0:T(128)S(1)}, f32[12]{0:T(128)S(1)}) all-reduce(f32[12]{0:T(128)S(1)} %get-tuple-element.429, f32[12]{0:T(128)S(1)} %get-tuple-element.428), channel_id=1, replica_groups=mesh['real'=2,'bx'=4,'by'=4] {'by'}, use_global_device_ids=true, to_apply=%region_4.5 | all-reduce | flops 24 | bytes 192 | tf_op jit(solution)/shard_map/psum | solution.py:155
  108.9 5.9 %all-reduce.28 = (f32[12]{0:T(128)S(1)}, f32[12]{0:T(128)S(1)}) all-reduce(f32[12]{0:T(128)S(1)} %get-tuple-element.352, f32[12]{0:T(128)S(1)} %get-tuple-element.353), channel_id=1, replica_groups=mesh['real'=2,'bx'=4,'by'=4] {'bx'}, use_global_device_ids=true, to_apply=%region_5.6 | all-reduce | flops 24 | bytes 192 | tf_op jit(solution)/shard_map/psum | solution.py:154
  127.9 2.8 %collective-permute-done.6 = f32[12,3,2,1,128]{4,0,3,2,1:T(8,128)S(1)} collective-permute-done((f32[12,3,2,1,128]{4,0,3,2,1:T(8,128)S(1)}, f32[12,3,2,1,128]{4,0,3,2,1:T(8,128)S(1)}, u32[]{:S(2)}, u32[]{:S(2)}) %collective-permute-start.6) | collective-permute-done | bytes 36896 | tf_op jit(solution)/shard_map/ppermute | solution.py:24
  135.0 25.6 %while.29 = (s32[]{:T(128)}, f32[3,4,3,3,9,129]{5,4,3,2,1,0:T(8,128)}, f32[3,4,3,3,9,129]{5,4,3,2,1,0:T(8,128)S(1)}, f32[8,3,8,3]{2,0,3,1:T(8,128)}, f32[2,8,128]{2,1,0:T(8,128)S(1)}, /*index=5*/s32[]{:T(128)}) while((s32[]{:T(128)}, f32[3,4,3,3,9,129]{5,4,3,2,1,0:T(8,128)}, f32[3,4,3,3,9,129]{5,4,3,2,1,0:T(8,128)S(1)}, ...), condition=%wide.region_10.11_spmd, body=%wide.region_9.10_spmd.sunk | while | flops 57112284 | bytes 15171361 | solution.py:71
  137.4 2.4 stack.111
  146.0 2.4 stack.111
  154.5 2.4 stack.111
  162.1 6.0 %collective-permute-start.8 = (f32[12,3,1,9,128]{4,0,3,2,1:T(8,128)S(1)}, f32[12,3,1,9,128]{4,0,3,2,1:T(8,128)S(1)}, u32[]{:S(2)}, u32[]{:S(2)}) collective-permute-start(f32[12,3,1,9,128]{4,0,3,2,1:T(8,128)S(1)} %copy.646), channel_id=1, source_target_pairs={{0,4},{4,8},{8,12},{1,5},{5,9},{9,13},{2,6},{6,10},{10,14},{3,7},{... | collective-permute-start | bytes 497672 | tf_op jit(solution)/shard_map/ppermute | solution.py:24
  169.9 5.5 %psum.55 = f32[]{:T(128)} all-reduce(f32[]{:T(128)} %get-tuple-element.356), channel_id=1, replica_groups=mesh['real'=2,'bx'=4,'by'=4] {'real'}, use_global_device_ids=true, to_apply=%region_15.16 | all-reduce | flops 1 | bytes 8 | tf_op jit(solution)/shard_map/psum | solution.py:177
  178.2 3.4 %collective-permute-start.9 = (f32[12,3,2,1,128]{4,0,3,2,1:T(8,128)S(1)}, f32[12,3,2,1,128]{4,0,3,2,1:T(8,128)S(1)}, u32[]{:S(2)}, u32[]{:S(2)}) collective-permute-start(f32[12,3,2,1,128]{4,0,3,2,1:T(8,128)S(1)} %pad_maximum_fusion.7), channel_id=1, source_target_pairs={{0,1},{1,2},{2,3},{4,5},{5,6},{6,7},{8,9},{9,10},{10,11},{12,13},{... | collective-permute-start | bytes 110600 | tf_op jit(solution)/shard_map/ppermute | solution.py:24
  185.5 60.8 %all-reduce.26 = (f32[1,36,36]{2,1,0:T(8,128)S(1)}, f32[1,36,36]{2,1,0:T(8,128)S(1)}) all-reduce(f32[1,36,36]{2,1,0:T(8,128)S(1)} %fusion.43, f32[1,36,36]{2,1,0:T(8,128)S(1)} %fusion.44), channel_id=1, replica_groups=mesh['real'=2,'bx'=4,'by'=4] {'bx','by'}, use_global_device_ids=true, to_apply=%region_11.12 | all-reduce | flops 2592 | bytes 20736 | tf_op jit(solution)/shard_map/psum | solution.py:169
  (322 shorter events, 98.0 us)
Async XLA Ops:
  7.2 170.0 %reduce-scatter.4.cloned.1.call-start = ((), (), s32[]{:S(2)}) async-start(), calls=%async_computation.1 | async-start | bytes 98304
  8.0 3.2 %collective-permute-start.4 = (f32[1,8,128]{2,1,0:T(8,128)S(1)}, f32[1,8,128]{2,1,0:T(8,128)S(1)}, u32[]{:S(2)}, u32[]{:S(2)}) collective-permute-start(f32[1,8,128]{2,1,0:T(8,128)S(1)} %slice.336), channel_id=1, source_target_pairs={{0,4},{4,8},{8,12},{1,5},{5,9},{9,13},{2,6},{6,10},{10,14},{3,7},{... | collective-permute-start | bytes 12296 | tf_op jit(solution)/shard_map/ppermute | solution.py:24
  11.2 15.7 %copy-start.26 = (f32[24,24]{1,0:T(8,128)S(1)}, f32[24,24]{1,0:T(8,128)}, u32[]{:S(2)}) copy-start(f32[24,24]{1,0:T(8,128)} %param.14) | copy-start | bytes 6916
  11.2 5.7 %collective-permute-start.5 = (f32[3,1,128]{2,1,0:T(1,128)S(1)}, f32[3,1,128]{2,1,0:T(1,128)S(1)}, u32[]{:S(2)}, u32[]{:S(2)}) collective-permute-start(f32[3,1,128]{2,1,0:T(1,128)S(1)} %pad_maximum_fusion.8), channel_id=1, source_target_pairs={{0,1},{1,2},{2,3},{4,5},{5,6},{6,7},{8,9},{9,10},{10,11},{12,13},{... | collective-permute-start | bytes 4616 | tf_op jit(solution)/shard_map/ppermute | solution.py:24
  17.0 10.2 %copy-start = (f32[1,12,3,2,8,128]{5,4,3,2,1,0:T(8,128)S(1)}, f32[1,12,3,2,8,128]{5,4,3,2,1,0:T(8,128)}, u32[]{:S(2)}) copy-start(f32[1,12,3,2,8,128]{5,4,3,2,1,0:T(8,128)} %param.12) | copy-start | bytes 884740
  17.0 10.2 %copy-start.1 = (f32[1,12,3,2,8,128]{5,4,3,2,1,0:T(8,128)S(1)}, f32[1,12,3,2,8,128]{5,4,3,2,1,0:T(8,128)}, u32[]{:S(2)}) copy-start(f32[1,12,3,2,8,128]{5,4,3,2,1,0:T(8,128)} %param.13) | copy-start | bytes 884740
  18.3 7.2 %collective-permute-start = (f32[24,3,2,1,128]{4,0,3,2,1:T(8,128)S(1)}, f32[24,3,2,1,128]{4,0,3,2,1:T(8,128)S(1)}, u32[]{:S(2)}, u32[]{:S(2)}) collective-permute-start(f32[24,3,2,1,128]{4,0,3,2,1:T(8,128)S(1)} %pad_maximum_fusion.6), channel_id=1, source_target_pairs={{1,0},{2,1},{3,2},{5,4},{6,5},{7,6},{9,8},{10,9},{11,10},{13,12},{... | collective-permute-start | bytes 221192 | tf_op jit(solution)/shard_map/ppermute | solution.py:24
  25.6 3.5 %collective-permute-start.1 = (f32[24,3,1,9,128]{4,0,3,2,1:T(8,128)S(1)}, f32[24,3,1,9,128]{4,0,3,2,1:T(8,128)S(1)}, u32[]{:S(2)}, u32[]{:S(2)}) collective-permute-start(f32[24,3,1,9,128]{4,0,3,2,1:T(8,128)S(1)} %pad_maximum_fusion.2), channel_id=1, source_target_pairs={{4,0},{8,4},{12,8},{5,1},{9,5},{13,9},{6,2},{10,6},{14,10},{7,3},{... | collective-permute-start | bytes 995336 | tf_op jit(solution)/shard_map/ppermute | solution.py:24
  78.6 12.5 %collective-permute-start.2 = (f32[24,3,1,9,128]{4,0,3,2,1:T(8,128)S(1)}, f32[24,3,1,9,128]{4,0,3,2,1:T(8,128)S(1)}, u32[]{:S(2)}, u32[]{:S(2)}) collective-permute-start(f32[24,3,1,9,128]{4,0,3,2,1:T(8,128)S(1)} %copy.643), channel_id=1, source_target_pairs={{0,4},{4,8},{8,12},{1,5},{5,9},{9,13},{2,6},{6,10},{10,14},{3,7},{... | collective-permute-start | bytes 995336 | tf_op jit(solution)/shard_map/ppermute | solution.py:24
  91.3 5.9 %collective-permute-start.3 = (f32[24,3,2,1,128]{4,0,3,2,1:T(8,128)S(1)}, f32[24,3,2,1,128]{4,0,3,2,1:T(8,128)S(1)}, u32[]{:S(2)}, u32[]{:S(2)}) collective-permute-start(f32[24,3,2,1,128]{4,0,3,2,1:T(8,128)S(1)} %pad_maximum_fusion.5), channel_id=1, source_target_pairs={{0,1},{1,2},{2,3},{4,5},{5,6},{6,7},{8,9},{9,10},{10,11},{12,13},{... | collective-permute-start | bytes 221192 | tf_op jit(solution)/shard_map/ppermute | solution.py:24
  96.6 18.9 %copy-start.25 = (f32[1,3,2,8,128]{4,3,2,1,0:T(8,128)S(1)}, f32[1,3,2,8,128]{4,3,2,1,0:T(8,128)}, u32[]{:S(2)}) copy-start(f32[1,3,2,8,128]{4,3,2,1,0:T(8,128)} %param.15) | copy-start | bytes 73732
  124.8 6.0 %collective-permute-start.6 = (f32[12,3,2,1,128]{4,0,3,2,1:T(8,128)S(1)}, f32[12,3,2,1,128]{4,0,3,2,1:T(8,128)S(1)}, u32[]{:S(2)}, u32[]{:S(2)}) collective-permute-start(f32[12,3,2,1,128]{4,0,3,2,1:T(8,128)S(1)} %slice.339), channel_id=1, source_target_pairs={{1,0},{2,1},{3,2},{5,4},{6,5},{7,6},{9,8},{10,9},{11,10},{13,12},{... | collective-permute-start | bytes 110600 | tf_op jit(solution)/shard_map/ppermute | solution.py:24
  130.8 3.8 %collective-permute-start.7 = (f32[12,3,1,9,128]{4,0,3,2,1:T(8,128)S(1)}, f32[12,3,1,9,128]{4,0,3,2,1:T(8,128)S(1)}, u32[]{:S(2)}, u32[]{:S(2)}) collective-permute-start(f32[12,3,1,9,128]{4,0,3,2,1:T(8,128)S(1)} %pad_maximum_fusion.4), channel_id=1, source_target_pairs={{4,0},{8,4},{12,8},{5,1},{9,5},{13,9},{6,2},{10,6},{14,10},{7,3},{... | collective-permute-start | bytes 497672 | tf_op jit(solution)/shard_map/ppermute | solution.py:24
  160.6 9.0 %copy-start.7 = (f32[12,12]{1,0:T(8,128)S(1)}, f32[12,12]{1,0:T(8,128)}, u32[]{:S(2)}) copy-start(f32[12,12]{1,0:T(8,128)} %convolution_bitcast_fusion.1) | copy-start | bytes 1732
  160.6 9.0 %copy-start.8 = (f32[12,12]{1,0:T(8,128)S(1)}, f32[12,12]{1,0:T(8,128)}, u32[]{:S(2)}) copy-start(f32[12,12]{1,0:T(8,128)} %convolution_bitcast_fusion.3) | copy-start | bytes 1732
  160.6 9.1 %copy-start.9 = (f32[12,12]{1,0:T(8,128)S(1)}, f32[12,12]{1,0:T(8,128)}, u32[]{:S(2)}) copy-start(f32[12,12]{1,0:T(8,128)} %convolution_bitcast_fusion.7) | copy-start | bytes 1732
  160.7 9.1 %copy-start.10 = (f32[12,12]{1,0:T(8,128)S(1)}, f32[12,12]{1,0:T(8,128)}, u32[]{:S(2)}) copy-start(f32[12,12]{1,0:T(8,128)} %convolution_bitcast_fusion.9) | copy-start | bytes 1732
  160.7 9.1 %copy-start.16 = (f32[12,12]{1,0:T(8,128)S(1)}, f32[12,12]{1,0:T(8,128)}, u32[]{:S(2)}) copy-start(f32[12,12]{1,0:T(8,128)} %convolution_bitcast_fusion.2) | copy-start | bytes 1732
  160.7 9.1 %copy-start.17 = (f32[12,12]{1,0:T(8,128)S(1)}, f32[12,12]{1,0:T(8,128)}, u32[]{:S(2)}) copy-start(f32[12,12]{1,0:T(8,128)} %convolution_bitcast_fusion.4) | copy-start | bytes 1732
  160.7 9.1 %copy-start.18 = (f32[12,12]{1,0:T(8,128)S(1)}, f32[12,12]{1,0:T(8,128)}, u32[]{:S(2)}) copy-start(f32[12,12]{1,0:T(8,128)} %convolution_bitcast_fusion.6) | copy-start | bytes 1732
  160.7 9.1 %copy-start.19 = (f32[12,12]{1,0:T(8,128)S(1)}, f32[12,12]{1,0:T(8,128)}, u32[]{:S(2)}) copy-start(f32[12,12]{1,0:T(8,128)} %convolution_bitcast_fusion.8) | copy-start | bytes 1732
  160.7 9.1 %copy-start.20 = (f32[12,12]{1,0:T(8,128)S(1)}, f32[12,12]{1,0:T(8,128)}, u32[]{:S(2)}) copy-start(f32[12,12]{1,0:T(8,128)} %convolution_bitcast_fusion.5) | copy-start | bytes 1732
  162.1 16.0 %collective-permute-start.8 = (f32[12,3,1,9,128]{4,0,3,2,1:T(8,128)S(1)}, f32[12,3,1,9,128]{4,0,3,2,1:T(8,128)S(1)}, u32[]{:S(2)}, u32[]{:S(2)}) collective-permute-start(f32[12,3,1,9,128]{4,0,3,2,1:T(8,128)S(1)} %copy.646), channel_id=1, source_target_pairs={{0,4},{4,8},{8,12},{1,5},{5,9},{9,13},{2,6},{6,10},{10,14},{3,7},{... | collective-permute-start | bytes 497672 | tf_op jit(solution)/shard_map/ppermute | solution.py:24
  178.2 5.1 %collective-permute-start.9 = (f32[12,3,2,1,128]{4,0,3,2,1:T(8,128)S(1)}, f32[12,3,2,1,128]{4,0,3,2,1:T(8,128)S(1)}, u32[]{:S(2)}, u32[]{:S(2)}) collective-permute-start(f32[12,3,2,1,128]{4,0,3,2,1:T(8,128)S(1)} %pad_maximum_fusion.7), channel_id=1, source_target_pairs={{0,1},{1,2},{2,3},{4,5},{5,6},{6,7},{8,9},{9,10},{10,11},{12,13},{... | collective-permute-start | bytes 110600 | tf_op jit(solution)/shard_map/ppermute | solution.py:24
  (18 other events, 61.5 us)
Sparse Core Ops, SparseCore 0:
  169.8 7.2 reduce-scatter.3
